TPU v7x, 32 devices: a whole 2x2x4 slice. The times are simulated.
32 devices in a mesh: freq: 2 (over y), harm: 4 (over z), wall: 4 (over x, core).
Axes of the slice: x: 2, y: 2, z: 4, core: 2. Of those that a mesh axis runs over, the one named last changes fastest.
Arguments:
- sketch: bfloat16 [32, 1024, 128], P(('freq', 'harm'), 'wall'), parts along dimension 0, may hold values from -48 to 48
- inverse_blocks: bfloat16 [32, 1024, 1024], P(('freq', 'harm'), 'wall'), parts along dimension 0, may hold values from -0.1875 to 0.1875
- couple_up: bfloat16 [8, 1024, 1024], P('freq', 'wall'), parts along dimension 0, may hold values from -0.03125 to 0.03125
- couple_down: bfloat16 [8, 1024, 1024], P('freq', 'wall'), parts along dimension 0, may hold values from -0.03125 to 0.03125
- strip_harmonics: int32 [8], P('freq'), parts along dimension 0, may hold values from 0 to 3
Outputs:
- basis: float32 [32, 1024, 128], P(('freq', 'harm'), 'wall'), parts along dimension 0
- triangle: float32 [256, 128], P('freq'), parts along dimension 0
There are 2 independent parts, one for each index of `freq`. A program takes and returns all parts, laid end to end along the dimension named above; each array names one. Nothing has to cross between parts.
Inputs may be any that keep to these rules, and one draw needn't show every extreme that they name: `strip_harmonics`: each entry one of 0 to 3; entries may repeat.
All inputs are finite; a program needn't handle non-finite values.
Results may differ from a plain program's by a relative error of at most 0.0045.
Values may be sent and summed in bfloat16 or wider, within the bound.
A program may use at most 64 MiB of HBM per device.

v0:
```python
import functools

import jax
import jax.numpy as jnp
from jax import lax
from jax.experimental import pallas as pl
from jax.experimental.pallas import tpu as pltpu
from jax.sharding import PartitionSpec as P

BAND = 4
SWEEPS = 3
MESH = pl.DeviceIdType.MESH


def flip(index, bit):
    return index + bit - 2 * bit * (lax.div(index, bit) % 2)


def bits_of(count):
    return [1 << b for b in range(count.bit_length() - 1)]


def visit_order(count):
    order = []
    for i in range((count + 1) // 2):
        order += [i] if count - 1 - i == i else [i, count - 1 - i]
    return order


def sweep_kernel(
    walls, harms, strip, sketch, inverse, up, down, sampled, gram,
    pieces, inverse_v, couple_v, products, partial, halo_out, halo_in,
    whole, summed, gathered, gram_out, gram_in,
    load_sem, recv_sem, send_sem, halo_send, halo_recv, gram_send, gram_recv,
):
    count, rows, width = sketch.shape
    w = lax.axis_index("wall")
    z = lax.axis_index("harm")
    prev, following = (z + harms - 1) % harms, (z + 1) % harms
    wall_bits, harm_bits = bits_of(walls), bits_of(harms)
    order = visit_order(count)

    near = min(4, harms)
    butterfly = [("wall", flip(w, b)) for b in wall_bits if b > 1]
    butterfly += [("harm", flip(z, b)) for b in harm_bits if b >= near]
    greet = [{"wall": flip(w, b)} for b in wall_bits]
    greet += [{"harm": flip(z, b)} for b in harm_bits if b >= near]
    greet += [{"harm": z - z % near + (z % near + d) % near} for d in range(1, near)]
    greet += [{"harm": prev}, {"harm": following}]
    barrier = pltpu.get_barrier_semaphore()

    loads = [
        pltpu.make_async_copy(inverse.at[h], inverse_v.at[h], load_sem.at[h]) for h in order
    ]
    loads += [
        pltpu.make_async_copy(up, couple_v.at[pl.ds(0, BAND)], load_sem.at[count]),
        pltpu.make_async_copy(down, couple_v.at[pl.ds(BAND, BAND)], load_sem.at[count + 1]),
    ]

    def block(g, h, m):
        source = w
        for b in wall_bits:
            if m & b:
                source = flip(source, b)
        return pieces.at[g, h, pl.ds(pl.multiple_of(source * rows, rows), rows)]

    own_copies = [
        pltpu.make_async_copy(sketch.at[h], block(0, h, 0), load_sem.at[count + 2 + h])
        for h in range(count)
    ]
    for copy in own_copies:
        copy.start()
    for peer in greet:
        pl.semaphore_signal(barrier, inc=1, device_id=peer, device_id_type=MESH)
    for copy in loads:
        copy.start()
    pl.semaphore_wait(barrier, len(greet))

    def hop(g, h, m, bit):
        return pltpu.make_async_remote_copy(
            src_ref=block(g, h, m), dst_ref=block(g, h, m),
            send_sem=send_sem.at[h, m + bit], recv_sem=recv_sem.at[g, h, m + bit],
            device_id={"wall": flip(w, bit)}, device_id_type=MESH,
        )

    def arrival(g, h, m):
        low = m & -m
        return pltpu.make_async_remote_copy(
            src_ref=block(g, h, m), dst_ref=block(g, h, m),
            send_sem=send_sem.at[h, m], recv_sem=recv_sem.at[g, h, m],
            device_id={"wall": flip(w, low)}, device_id_type=MESH,
        )

    def send_own(g, h):
        for bit in reversed(wall_bits):
            hop(g, h, 0, bit).start()

    def relay(g, h):
        for m in sorted(range(2, walls, 2), key=lambda m: -(m & -m)):
            arrival(g, h, m).wait_recv()
            for bit in reversed(wall_bits):
                if bit < (m & -m):
                    hop(g, h, m, bit).start()

    def finish(g, h):
        for m in range(1, walls, 2):
            arrival(g, h, m).wait_recv()

    def collect(g, h):
        relay(g, h)
        finish(g, h)

    def settle(g, h):
        for m in range(1, walls):
            arrival(g, h, m).wait_send()

    def apply_inverse(g, h):
        return jnp.dot(inverse_v[h], pieces[g, h], preferred_element_type=jnp.float32)

    def store_own(g, h, value):
        pieces[g, h, pl.ds(pl.multiple_of(w * rows, rows), rows), :] = value

    for h in order:
        own_copies[h].wait()
        send_own(0, h)

    blank = jnp.zeros((rows, width), jnp.float32)

    @pl.loop(0, 2 * BAND)
    def _(j):
        for slot in range(BAND):
            products[j, slot] = blank
            products[j, count + BAND + slot] = blank

    for i, h in enumerate(order):
        collect(0, h)
        loads[i].wait()
        state = apply_inverse(0, h).astype(jnp.bfloat16)
        settle(0, h)
        store_own(1, h, state)
        send_own(1, h)
    loads[count].wait()
    loads[count + 1].wait()

    offsets = [strip[j] + 1 for j in range(BAND)]

    def halo(s, side, i):
        return pltpu.make_async_remote_copy(
            src_ref=halo_out.at[s, side, i], dst_ref=halo_in.at[s, side, i],
            send_sem=halo_send.at[side, i], recv_sem=halo_recv.at[s, side, i],
            device_id={"harm": prev if side == 0 else following}, device_id_type=MESH,
        )

    def from_below(t):
        total = products[0, t - offsets[0] + BAND]
        for j in range(1, BAND):
            total = total + products[j, t - offsets[j] + BAND]
        return total

    def from_above(t):
        total = products[BAND, t + offsets[0] + BAND]
        for j in range(1, BAND):
            total = total + products[BAND + j, t + offsets[j] + BAND]
        return total

    slots = []
    for i in range(BAND):
        slots.append((1, i, {count + i - o for o in range(1, BAND + 1)}))
        slots.append((0, BAND - 1 - i, {o - 1 - i for o in range(1, BAND + 1)}))
    slots = [(side, i, {h for h in need if 0 <= h < count}) for side, i, need in slots]

    for s in range(SWEEPS):
        g_state, g_rhs = 1 + 2 * s, 2 + 2 * s
        done, sent = set(), set()
        for start in range(0, count, 2):
            group, later = order[start : start + 2], order[start + 2 : start + 4]
            for h in group:
                if start == 0:
                    relay(g_state, h)
            for h in group:
                finish(g_state, h)

            def couple(j):
                state = jnp.concatenate([pieces[g_state, h] for h in group], axis=1)
                both = jnp.dot(couple_v[j], state, preferred_element_type=jnp.float32)
                for at, h in enumerate(group):
                    products[j, h + BAND] = both[:, at * width : (at + 1) * width]

            pl.loop(0, BAND, unroll=BAND)(couple)
            for h in later:
                relay(g_state, h)
            pl.loop(BAND, 2 * BAND, unroll=BAND)(couple)
            done |= set(group)
            for side, i, need in slots:
                if (side, i) not in sent and need <= done:
                    sent.add((side, i))
                    value = from_above(i - BAND) if side == 0 else from_below(count + i)
                    halo_out[s, side, i] = value.astype(jnp.bfloat16)
                    halo(s, side, i).start()
        for h in order:
            settle(g_state, h)
            own = pieces[0, h, pl.ds(pl.multiple_of(w * rows, rows), rows), :]
            partial[h] = own.astype(jnp.float32) - (from_below(h) + from_above(h))
        for h in order:
            rhs = partial[h]
            if h < BAND:
                halo(s, 1, h).wait_recv()
                rhs = rhs - halo_in[s, 1, h].astype(jnp.float32)
            if h >= count - BAND:
                i = h - count + BAND
                halo(s, 0, i).wait_recv()
                rhs = rhs - halo_in[s, 0, i].astype(jnp.float32)
            store_own(g_rhs, h, rhs.astype(jnp.bfloat16))
            send_own(g_rhs, h)
        for side in range(2):
            for i in range(BAND):
                halo(s, side, i).wait_send()
        total = jnp.zeros((width, width), jnp.float32)
        for h in order:
            collect(g_rhs, h)
            result = apply_inverse(g_rhs, h)
            settle(g_rhs, h)
            if s < SWEEPS - 1:
                store_own(g_rhs + 1, h, result.astype(jnp.bfloat16))
                send_own(g_rhs + 1, h)
            else:
                sampled[h] = result
                total = total + lax.dot_general(
                    result, result, (((0,), (0,)), ((), ())),
                    precision=lax.Precision.HIGHEST, preferred_element_type=jnp.float32,
                )

    part = width // 2
    mine, theirs = (w % 2) * part, (1 - w % 2) * part

    def swap(stage, source, target, peer):
        copy = pltpu.make_async_remote_copy(
            src_ref=source, dst_ref=target, send_sem=gram_send.at[stage],
            recv_sem=gram_recv.at[stage], device_id=peer, device_id_type=MESH,
        )
        copy.start()
        return copy

    whole[...] = total
    swap(
        0, whole.at[pl.ds(pl.multiple_of(theirs, part), part)], gram_in.at[0], {"wall": flip(w, 1)}
    ).wait()
    half = whole[pl.ds(pl.multiple_of(mine, part), part), :] + gram_in[0]
    stage = 1
    for axis, peer in butterfly:
        gram_out[stage] = half
        swap(stage, gram_out.at[stage], gram_in.at[stage], {axis: peer}).wait()
        half = half + gram_in[stage]
        stage += 1
    me = z % near
    gathered[me] = half
    copies = [
        swap(stage + d - 1, gathered.at[me], gathered.at[me], {"harm": z - me + (me + d) % near})
        for d in range(1, near)
    ]
    for copy in copies:
        copy.wait()
    half = gathered[0]
    for d in range(1, near):
        half = half + gathered[d]
    stage += near - 1
    half = half / (harms * walls * count * rows)
    place = pl.ds(pl.multiple_of(mine, part), part)
    summed[place, :] = half
    swap(stage, summed.at[place], summed.at[place], {"wall": flip(w, 1)}).wait()
    gram[...] = summed[...]


def factor_kernel(sampled, gram, basis, triangle, work, inverse_lower):
    count, rows, width = sampled.shape
    panel = 8
    row_at = lax.broadcasted_iota(jnp.int32, (width, width), 0)
    col_at = lax.broadcasted_iota(jnp.int32, (width, width), 1)
    at = lax.broadcasted_iota(jnp.int32, (panel, width), 0)
    work[...] = gram[...]
    inverse_lower[...] = jnp.where(row_at == col_at, 1.0, 0.0)

    def spread(value, i):
        return jnp.broadcast_to(value[i : i + 1, :], (panel, width))

    for low in range(0, width, panel):
        a = work[low : low + panel, :]
        x = inverse_lower[low : low + panel, :]
        columns = [
            jnp.broadcast_to(a[:, low + i : low + i + 1], (panel, width)) for i in range(panel)
        ]
        pivots = jnp.ones((panel, width), jnp.float32)
        for i in range(panel):
            pivot = spread(columns[i], i)
            pivots = jnp.where(at == i, pivot, pivots)
            factor = jnp.where(at > i, columns[i] * (1.0 / pivot), 0.0)
            for m in range(i + 1, panel):
                columns[m] = columns[m] - factor * spread(columns[m], i)
            a = a - factor * spread(a, i)
            x = x - factor * spread(x, i)
        unit = lax.rsqrt(pivots)
        a, x = a * unit, x * unit
        work[low : low + panel, :] = a
        inverse_lower[low : low + panel, :] = x
        if low + panel < width:
            change = lax.dot_general(
                a, jnp.concatenate([a, x], axis=1), (((0,), (0,)), ((), ())),
                precision=lax.Precision.HIGHEST, preferred_element_type=jnp.float32,
            )
            below = low + panel
            work[below:, :] = work[below:, :] - change[below:, :width]
            inverse_lower[below:, :] = inverse_lower[below:, :] - change[below:, width:]

    triangle[...] = jnp.where(row_at <= col_at, work[...], 0.0)
    for h in range(count):
        basis[h] = lax.dot_general(
            sampled[h], inverse_lower[...], (((1,), (1,)), ((), ())),
            precision=lax.Precision.HIGHEST, preferred_element_type=jnp.float32,
        )


def body(walls, harms, sketch, inverse_blocks, couple_up, couple_down, strip_harmonics):
    count, rows, width = sketch.shape
    size = rows * walls
    near = min(4, harms)
    stages = len(bits_of(walls)) + len(bits_of(harms // near)) + near
    gathers = 1 + 2 * SWEEPS
    vmem = pl.BlockSpec(memory_space=pltpu.VMEM)
    anywhere = pl.BlockSpec(memory_space=pl.ANY)
    sampled, gram = pl.pallas_call(
        functools.partial(sweep_kernel, walls, harms),
        out_shape=(
            jax.ShapeDtypeStruct((count, rows, width), jnp.float32),
            jax.ShapeDtypeStruct((width, width), jnp.float32),
        ),
        in_specs=[pl.BlockSpec(memory_space=pltpu.SMEM)] + [anywhere] * 4,
        out_specs=(vmem, vmem),
        scratch_shapes=[
            pltpu.VMEM((gathers, count, size, width), jnp.bfloat16),
            pltpu.VMEM((count, rows, size), jnp.bfloat16),
            pltpu.VMEM((2 * BAND, rows, size), jnp.bfloat16),
            pltpu.VMEM((2 * BAND, count + 2 * BAND, rows, width), jnp.float32),
            pltpu.VMEM((count, rows, width), jnp.float32),
            pltpu.VMEM((SWEEPS, 2, BAND, rows, width), jnp.bfloat16),
            pltpu.VMEM((SWEEPS, 2, BAND, rows, width), jnp.bfloat16),
            pltpu.VMEM((width, width), jnp.float32),
            pltpu.VMEM((width, width), jnp.float32),
            pltpu.VMEM((near, width // 2, width), jnp.float32),
            pltpu.VMEM((stages, width // 2, width), jnp.float32),
            pltpu.VMEM((stages, width // 2, width), jnp.float32),
            pltpu.SemaphoreType.DMA((2 * count + 2,)),
            pltpu.SemaphoreType.DMA((gathers, count, walls)),
            pltpu.SemaphoreType.DMA((count, walls)),
            pltpu.SemaphoreType.DMA((2, BAND)),
            pltpu.SemaphoreType.DMA((SWEEPS, 2, BAND)),
            pltpu.SemaphoreType.DMA((stages,)),
            pltpu.SemaphoreType.DMA((stages,)),
        ],
        compiler_params=pltpu.CompilerParams(
            collective_id=0, has_side_effects=True, vmem_limit_bytes=67043328
        ),
        name="sweeps",
    )(strip_harmonics, sketch, inverse_blocks, couple_up, couple_down)
    return pl.pallas_call(
        factor_kernel,
        out_shape=(
            jax.ShapeDtypeStruct((count, rows, width), jnp.float32),
            jax.ShapeDtypeStruct((width, width), jnp.float32),
        ),
        in_specs=[vmem, vmem],
        out_specs=(vmem, vmem),
        scratch_shapes=[pltpu.VMEM((width, width), jnp.float32)] * 2,
        name="factor",
    )(sampled, gram)


def solution(mesh):
    return jax.shard_map(
        functools.partial(body, mesh.shape["wall"], mesh.shape["harm"]),
        mesh=mesh,
        in_specs=(
            P(("freq", "harm"), "wall", None),
            P(("freq", "harm"), "wall", None),
            P("freq", "wall", None),
            P("freq", "wall", None),
            P("freq"),
        ),
        out_specs=(P(("freq", "harm"), "wall", None), P("freq", None)),
        check_vma=False,
    )
```

profile of v0, /device:TPU:0, one launch (start us, length us, event | category | flops | bytes accessed | tf_op | source)
XLA Modules:
  0.0 110.0 jit_solution(13791115353017443071)
XLA Ops:
  0.6 98.5 %sweeps.1 = (f32[4,256,128]{2,1,0:T(8,128)}, f32[128,128]{1,0:T(8,128)}) custom-call(s32[4]{0:T(128)} %strip.1, bf16[4,256,128]{2,1,0:T(8,128)(2,1)} %sketch.1, bf16[4,256,1024]{2,1,0:T(8,128)(2,1)} %inverse.1, bf16[4,256,1024]{2,1,0:T(8,128)(2,1)} %up.1, bf16[4,256,1024]{2,1,0:T(8,128)(2,1)} %down.1), custom_call_target="tpu_custom_call" | custom-call | tf_op jit(solution)/shard_map/sweeps/pallas_call | solution.py:330
  99.1 10.9 %factor.1 = (f32[4,256,128]{2,1,0:T(8,128)}, f32[128,128]{1,0:T(8,128)}) custom-call(f32[4,256,128]{2,1,0:T(8,128)} %get-tuple-element.4.sampled, f32[128,128]{1,0:T(8,128)} %get-tuple-element.5.gram), custom_call_target="tpu_custom_call" | custom-call | tf_op jit(solution)/shard_map/factor/pallas_call | solution.py:364
where the time goes:
time: 110 us
  Pallas kernels  109 us (99%)
    pallas_call x1, Pallas kernels, body(): pl.pallas_call(functools.partial(sweep_kernel, walls, harms), out_shape=(...  98.5 us
    pallas_call x1, Pallas kernels, body(): pl.pallas_call(factor_kernel, out_shape=(jax.ShapeDtypeStruct((count, row...  10.9 us

commit v1 on v0

--- a/solution.py
+++ b/solution.py
@@ -155,7 +155,8 @@
         total = products[0, t - offsets[0] + BAND]
         for j in range(1, BAND):
             total = total + products[j, t - offsets[j] + BAND]
-        return total
+        shift = offsets[0] * (width // 4)
+        return pltpu.roll(pltpu.roll(total, shift, 1), width - shift, 1)
 
     def from_above(t):
         total = products[BAND, t + offsets[0] + BAND]

time: 110 us -> 111 us (level)
  no operation moved by 1% of the time
where the time goes in v1:
time: 111 us; the launch traced here: 110 us
  Pallas kernels  110 us (99%)
    pallas_call x1, Pallas kernels, body(): pl.pallas_call(functools.partial(sweep_kernel, walls, harms), out_shape=(...  98.9 us
    pallas_call x1, Pallas kernels, body(): pl.pallas_call(factor_kernel, out_shape=(jax.ShapeDtypeStruct((count, row...  10.9 us

profile of v1, /device:TPU:0, one launch (start us, length us, event | category | flops | bytes accessed | tf_op | source)
XLA Modules:
  0.0 110.4 jit_solution(10168965510753360037)
XLA Ops:
  0.6 98.9 %sweeps.1 = (f32[4,256,128]{2,1,0:T(8,128)}, f32[128,128]{1,0:T(8,128)}) custom-call(s32[4]{0:T(128)} %strip.1, bf16[4,256,128]{2,1,0:T(8,128)(2,1)} %sketch.1, bf16[4,256,1024]{2,1,0:T(8,128)(2,1)} %inverse.1, bf16[4,256,1024]{2,1,0:T(8,128)(2,1)} %up.1, bf16[4,256,1024]{2,1,0:T(8,128)(2,1)} %down.1), custom_call_target="tpu_custom_call" | custom-call | tf_op jit(solution)/shard_map/sweeps/pallas_call | solution.py:331
  99.5 10.9 %factor.1 = (f32[4,256,128]{2,1,0:T(8,128)}, f32[128,128]{1,0:T(8,128)}) custom-call(f32[4,256,128]{2,1,0:T(8,128)} %get-tuple-element.4.sampled, f32[128,128]{1,0:T(8,128)} %get-tuple-element.5.gram), custom_call_target="tpu_custom_call" | custom-call | tf_op jit(solution)/shard_map/factor/pallas_call | solution.py:365

commit v2 on v0

v2 whole, which is shorter than its diff:
```python
import functools

import jax
import jax.numpy as jnp
from jax import lax
from jax.experimental import pallas as pl
from jax.experimental.pallas import tpu as pltpu
from jax.sharding import PartitionSpec as P

BAND = 4
SWEEPS = 3
MESH = pl.DeviceIdType.MESH


def flip(index, bit):
    return index + bit - 2 * bit * (lax.div(index, bit) % 2)


def bits_of(count):
    return [1 << b for b in range(count.bit_length() - 1)]


def plan(count):
    last = count - 1
    steps = []
    for s in range(-1, SWEEPS + 1):
        steps += [("couple", s, 0), ("relay rhs", s - 1, last)]
        steps += [("relay state", s, 1), ("solve", s - 1, last), ("couple", s, 1)]
        for c in range(2, count):
            steps += [("relay state", s, c), ("couple", s, c), ("correct", s, c - 2)]
        steps += [("relay rhs", s, 0), ("solve", s, 0)]
        for c in range(1, last):
            steps += [("correct", s, c + 1), ("relay rhs", s, c)]
            if c == last - 1:
                steps += [("relay state", s + 1, 0)]
            steps += [("solve", s, c)]
    def holds(step, s, c):
        if step == "relay state":
            return 0 <= s < SWEEPS
        return (-1 if step in ("relay rhs", "solve") else 0) <= s < SWEEPS
    return [entry for entry in steps if holds(*entry)]


def sweep_kernel(
    walls, harms, strip, sketch, inverse, up, down, sampled, gram,
    sketch_v, pieces, inverse_v, couple_v, partial, halo_out, halo_in,
    whole, summed, gathered, gram_out, gram_in,
    load_sem, recv_sem, send_sem, halo_send, halo_recv, gram_send, gram_recv,
):
    count, rows, width = sketch.shape
    lanes = width // count
    w = lax.axis_index("wall")
    z = lax.axis_index("harm")
    prev, following = (z + harms - 1) % harms, (z + 1) % harms
    wall_bits, harm_bits = bits_of(walls), bits_of(harms)
    lane = lax.broadcasted_iota(jnp.int32, (rows, width), 1)

    near = min(4, harms)
    butterfly = [("wall", flip(w, b)) for b in wall_bits if b > 1]
    butterfly += [("harm", flip(z, b)) for b in harm_bits if b >= near]
    greet = [{"wall": flip(w, b)} for b in wall_bits]
    greet += [{"harm": flip(z, b)} for b in harm_bits if b >= near]
    greet += [{"harm": z - z % near + (z % near + d) % near} for d in range(1, near)]
    greet += [{"harm": prev}, {"harm": following}]
    barrier = pltpu.get_barrier_semaphore()

    own_copy = pltpu.make_async_copy(sketch, sketch_v, load_sem.at[count + 2])
    own_copy.start()
    for peer in greet:
        pl.semaphore_signal(barrier, inc=1, device_id=peer, device_id_type=MESH)
    inverse_loads = [
        pltpu.make_async_copy(inverse.at[h], inverse_v.at[h], load_sem.at[h]) for h in range(count)
    ]
    couple_loads = [
        pltpu.make_async_copy(up, couple_v.at[pl.ds(0, BAND)], load_sem.at[count]),
        pltpu.make_async_copy(down, couple_v.at[pl.ds(BAND, BAND)], load_sem.at[count + 1]),
    ]
    for copy in inverse_loads + couple_loads:
        copy.start()

    def block(g, c, m):
        source = w
        for b in wall_bits:
            if m & b:
                source = flip(source, b)
        return pieces.at[g, c, pl.ds(pl.multiple_of(source * rows, rows), rows)]

    def hop(g, c, m, bit):
        return pltpu.make_async_remote_copy(
            src_ref=block(g, c, m), dst_ref=block(g, c, m),
            send_sem=send_sem.at[g, c, m + bit], recv_sem=recv_sem.at[g, c, m + bit],
            device_id={"wall": flip(w, bit)}, device_id_type=MESH,
        )

    def arrival(g, c, m):
        low = m & -m
        return pltpu.make_async_remote_copy(
            src_ref=block(g, c, m), dst_ref=block(g, c, m),
            send_sem=send_sem.at[g, c, m], recv_sem=recv_sem.at[g, c, m],
            device_id={"wall": flip(w, low)}, device_id_type=MESH,
        )

    def send_own(g, c):
        for bit in reversed(wall_bits):
            hop(g, c, 0, bit).start()

    def relay(g, c):
        for m in sorted(range(2, walls, 2), key=lambda m: -(m & -m)):
            arrival(g, c, m).wait_recv()
            for bit in reversed(wall_bits):
                if bit < (m & -m):
                    hop(g, c, m, bit).start()

    def finish(g, c):
        for m in range(1, walls, 2):
            arrival(g, c, m).wait_recv()

    def own(c):
        return pl.ds(pl.multiple_of(w * rows, rows), rows)

    def halo(s, side, c):
        return pltpu.make_async_remote_copy(
            src_ref=halo_out.at[s, side, c], dst_ref=halo_in.at[s, side, c],
            send_sem=halo_send.at[s, side, c], recv_sem=halo_recv.at[s, side, c],
            device_id={"harm": prev if side == 0 else following}, device_id_type=MESH,
        )

    def start(c):
        tile = None
        for h in range(count):
            turn = (h - c) % count * lanes
            source = sketch_v[h].astype(jnp.float32)
            source = source if turn == 0 else pltpu.roll(source, turn, 1)
            tile = source if tile is None else jnp.where(lane < h * lanes, tile, source)
        pieces[0, c, own(c), :] = tile.astype(jnp.bfloat16)
        send_own(0, c)

    shifts = [(strip[j] + 1) * lanes for j in range(BAND)]

    def couple(s, c):
        g = 2 * s + 1
        finish(g, c)
        local = pieces[0, c, own(c), :].astype(jnp.float32)
        away = jnp.zeros((rows, width), jnp.float32)
        for j in range(BAND):
            product = jnp.dot(couple_v[j], pieces[g, c], preferred_element_type=jnp.float32)
            product = pltpu.roll(product, lax.rem(shifts[j], width), 1)
            stays = lane >= shifts[j]
            local = local - jnp.where(stays, product, 0.0)
            away = away + jnp.where(stays, 0.0, product)
        halo_out[s, 1, c] = away.astype(jnp.bfloat16)
        halo(s, 1, c).start()
        away = jnp.zeros((rows, width), jnp.float32)
        for j in range(BAND):
            product = jnp.dot(couple_v[BAND + j], pieces[g, c], preferred_element_type=jnp.float32)
            product = pltpu.roll(product, width - shifts[j], 1)
            stays = lane < width - shifts[j]
            local = local - jnp.where(stays, product, 0.0)
            away = away + jnp.where(stays, 0.0, product)
        halo_out[s, 0, c] = away.astype(jnp.bfloat16)
        halo(s, 0, c).start()
        partial[c] = local

    def correct(s, c):
        rhs = partial[c]
        for side in (1, 0):
            halo(s, side, c).wait_recv()
            rhs = rhs - halo_in[s, side, c].astype(jnp.float32)
        pieces[2 * s + 2, c, own(c), :] = rhs.astype(jnp.bfloat16)
        send_own(2 * s + 2, c)

    def solve(s, c):
        g = 2 * s + 2
        finish(g, c)
        result = None
        for h in range(count):
            product = jnp.dot(inverse_v[h], pieces[g, c], preferred_element_type=jnp.float32)
            result = product if result is None else jnp.where(lane < h * lanes, result, product)
        if s < SWEEPS - 1:
            pieces[g + 1, c, own(c), :] = result.astype(jnp.bfloat16)
            send_own(g + 1, c)
        else:
            partial[c] = result

    pl.semaphore_wait(barrier, len(greet))
    own_copy.wait()
    for c in range(count):
        start(c)
    ready = set()
    for step, s, c in plan(count):
        if step == "solve" and "inverse" not in ready:
            ready.add("inverse")
            for copy in inverse_loads:
                copy.wait()
        if step == "couple" and "couple" not in ready:
            ready.add("couple")
            for copy in couple_loads:
                copy.wait()
        if step == "relay rhs":
            relay(2 * s + 2, c)
        elif step == "relay state":
            relay(2 * s + 1, c)
        else:
            {"solve": solve, "couple": couple, "correct": correct}[step](s, c)

    total = jnp.zeros((width, width), jnp.float32)
    for h in range(count):
        tile = None
        for c in range(count):
            turn = (c - h) % count * lanes
            source = partial[c] if turn == 0 else pltpu.roll(partial[c], turn, 1)
            tile = source if tile is None else jnp.where(lane < c * lanes, tile, source)
        sampled[h] = tile
        total = total + lax.dot_general(
            tile, tile, (((0,), (0,)), ((), ())),
            precision=lax.Precision.HIGHEST, preferred_element_type=jnp.float32,
        )

    part = width // 2
    mine, theirs = (w % 2) * part, (1 - w % 2) * part

    def swap(stage, source, target, peer):
        copy = pltpu.make_async_remote_copy(
            src_ref=source, dst_ref=target, send_sem=gram_send.at[stage],
            recv_sem=gram_recv.at[stage], device_id=peer, device_id_type=MESH,
        )
        copy.start()
        return copy

    whole[...] = total
    swap(
        0, whole.at[pl.ds(pl.multiple_of(theirs, part), part)], gram_in.at[0], {"wall": flip(w, 1)}
    ).wait()
    half = whole[pl.ds(pl.multiple_of(mine, part), part), :] + gram_in[0]
    stage = 1
    for axis, peer in butterfly:
        gram_out[stage] = half
        swap(stage, gram_out.at[stage], gram_in.at[stage], {axis: peer}).wait()
        half = half + gram_in[stage]
        stage += 1
    me = z % near
    gathered[me] = half
    copies = [
        swap(stage + d - 1, gathered.at[me], gathered.at[me], {"harm": z - me + (me + d) % near})
        for d in range(1, near)
    ]
    for copy in copies:
        copy.wait()
    half = gathered[0]
    for d in range(1, near):
        half = half + gathered[d]
    stage += near - 1
    half = half / (harms * walls * count * rows)
    place = pl.ds(pl.multiple_of(mine, part), part)
    summed[place, :] = half
    swap(stage, summed.at[place], summed.at[place], {"wall": flip(w, 1)}).wait()
    gram[...] = summed[...]
    for c in range(count):
        for g in range(2 * SWEEPS + 1):
            for m in range(1, walls):
                arrival(g, c, m).wait_send()
        for s in range(SWEEPS):
            for side in range(2):
                halo(s, side, c).wait_send()


def factor_kernel(sampled, gram, basis, triangle, work, inverse_lower):
    count, rows, width = sampled.shape
    panel = 8
    row_at = lax.broadcasted_iota(jnp.int32, (width, width), 0)
    col_at = lax.broadcasted_iota(jnp.int32, (width, width), 1)
    at = lax.broadcasted_iota(jnp.int32, (panel, width), 0)
    work[...] = gram[...]
    inverse_lower[...] = jnp.where(row_at == col_at, 1.0, 0.0)

    def spread(value, i):
        return jnp.broadcast_to(value[i : i + 1, :], (panel, width))

    for low in range(0, width, panel):
        a = work[low : low + panel, :]
        x = inverse_lower[low : low + panel, :]
        columns = [
            jnp.broadcast_to(a[:, low + i : low + i + 1], (panel, width)) for i in range(panel)
        ]
        pivots = jnp.ones((panel, width), jnp.float32)
        for i in range(panel):
            pivot = spread(columns[i], i)
            pivots = jnp.where(at == i, pivot, pivots)
            factor = jnp.where(at > i, columns[i] * (1.0 / pivot), 0.0)
            for m in range(i + 1, panel):
                columns[m] = columns[m] - factor * spread(columns[m], i)
            a = a - factor * spread(a, i)
            x = x - factor * spread(x, i)
        unit = lax.rsqrt(pivots)
        a, x = a * unit, x * unit
        work[low : low + panel, :] = a
        inverse_lower[low : low + panel, :] = x
        if low + panel < width:
            change = lax.dot_general(
                a, jnp.concatenate([a, x], axis=1), (((0,), (0,)), ((), ())),
                precision=lax.Precision.HIGHEST, preferred_element_type=jnp.float32,
            )
            below = low + panel
            work[below:, :] = work[below:, :] - change[below:, :width]
            inverse_lower[below:, :] = inverse_lower[below:, :] - change[below:, width:]

    triangle[...] = jnp.where(row_at <= col_at, work[...], 0.0)
    for h in range(count):
        basis[h] = lax.dot_general(
            sampled[h], inverse_lower[...], (((1,), (1,)), ((), ())),
            precision=lax.Precision.HIGHEST, preferred_element_type=jnp.float32,
        )


def body(walls, harms, sketch, inverse_blocks, couple_up, couple_down, strip_harmonics):
    count, rows, width = sketch.shape
    size = rows * walls
    near = min(4, harms)
    stages = len(bits_of(walls)) + len(bits_of(harms // near)) + near
    gathers = 1 + 2 * SWEEPS
    vmem = pl.BlockSpec(memory_space=pltpu.VMEM)
    anywhere = pl.BlockSpec(memory_space=pl.ANY)
    sampled, gram = pl.pallas_call(
        functools.partial(sweep_kernel, walls, harms),
        out_shape=(
            jax.ShapeDtypeStruct((count, rows, width), jnp.float32),
            jax.ShapeDtypeStruct((width, width), jnp.float32),
        ),
        in_specs=[pl.BlockSpec(memory_space=pltpu.SMEM)] + [anywhere] * 4,
        out_specs=(vmem, vmem),
        scratch_shapes=[
            pltpu.VMEM((count, rows, width), jnp.bfloat16),
            pltpu.VMEM((gathers, count, size, width), jnp.bfloat16),
            pltpu.VMEM((count, rows, size), jnp.bfloat16),
            pltpu.VMEM((2 * BAND, rows, size), jnp.bfloat16),
            pltpu.VMEM((count, rows, width), jnp.float32),
            pltpu.VMEM((SWEEPS, 2, count, rows, width), jnp.bfloat16),
            pltpu.VMEM((SWEEPS, 2, count, rows, width), jnp.bfloat16),
            pltpu.VMEM((width, width), jnp.float32),
            pltpu.VMEM((width, width), jnp.float32),
            pltpu.VMEM((near, width // 2, width), jnp.float32),
            pltpu.VMEM((stages, width // 2, width), jnp.float32),
            pltpu.VMEM((stages, width // 2, width), jnp.float32),
            pltpu.SemaphoreType.DMA((count + 3,)),
            pltpu.SemaphoreType.DMA((gathers, count, walls)),
            pltpu.SemaphoreType.DMA((gathers, count, walls)),
            pltpu.SemaphoreType.DMA((SWEEPS, 2, count)),
            pltpu.SemaphoreType.DMA((SWEEPS, 2, count)),
            pltpu.SemaphoreType.DMA((stages,)),
            pltpu.SemaphoreType.DMA((stages,)),
        ],
        compiler_params=pltpu.CompilerParams(
            collective_id=0, has_side_effects=True, vmem_limit_bytes=67043328
        ),
        name="sweeps",
    )(strip_harmonics, sketch, inverse_blocks, couple_up, couple_down)
    return pl.pallas_call(
        factor_kernel,
        out_shape=(
            jax.ShapeDtypeStruct((count, rows, width), jnp.float32),
            jax.ShapeDtypeStruct((width, width), jnp.float32),
        ),
        in_specs=[vmem, vmem],
        out_specs=(vmem, vmem),
        scratch_shapes=[pltpu.VMEM((width, width), jnp.float32)] * 2,
        name="factor",
    )(sampled, gram)


def solution(mesh):
    return jax.shard_map(
        functools.partial(body, mesh.shape["wall"], mesh.shape["harm"]),
        mesh=mesh,
        in_specs=(
            P(("freq", "harm"), "wall", None),
            P(("freq", "harm"), "wall", None),
            P("freq", "wall", None),
            P("freq", "wall", None),
            P("freq"),
        ),
        out_specs=(P(("freq", "harm"), "wall", None), P("freq", None)),
        check_vma=False,
    )
```

time: 110 us -> 99.1 us (0.901)
  Pallas kernels: 109 us -> 98.3 us
    pallas_call x1, Pallas kernels: 98.5 us -> 87.5 us  [body(): pl.pallas_call(functools.partial(sweep_kernel, walls, harms), out_shape=(...]
where the time goes in v2:
time: 99.1 us; the launch traced here: 99 us
  Pallas kernels  98.3 us (99%)
    pallas_call x1, Pallas kernels, body(): pl.pallas_call(functools.partial(sweep_kernel, walls, harms), out_shape=(...  87.5 us
    pallas_call x1, Pallas kernels, body(): pl.pallas_call(factor_kernel, out_shape=(jax.ShapeDtypeStruct((count, row...  10.9 us

profile of v2, /device:TPU:0, one launch (start us, length us, event | category | flops | bytes accessed | tf_op | source)
XLA Modules:
  0.0 99.0 jit_solution(11236674927974829476)
XLA Ops:
  0.6 87.5 %sweeps.1 = (f32[4,256,128]{2,1,0:T(8,128)}, f32[128,128]{1,0:T(8,128)}) custom-call(s32[4]{0:T(128)} %strip.1, bf16[4,256,128]{2,1,0:T(8,128)(2,1)} %sketch.1, bf16[4,256,1024]{2,1,0:T(8,128)(2,1)} %inverse.1, bf16[4,256,1024]{2,1,0:T(8,128)(2,1)} %up.1, bf16[4,256,1024]{2,1,0:T(8,128)(2,1)} %down.1), custom_call_target="tpu_custom_call" | custom-call | tf_op jit(solution)/shard_map/sweeps/pallas_call | solution.py:323
  88.1 10.9 %factor.1 = (f32[4,256,128]{2,1,0:T(8,128)}, f32[128,128]{1,0:T(8,128)}) custom-call(f32[4,256,128]{2,1,0:T(8,128)} %get-tuple-element.4.sampled, f32[128,128]{1,0:T(8,128)} %get-tuple-element.5.gram), custom_call_target="tpu_custom_call" | custom-call | tf_op jit(solution)/shard_map/factor/pallas_call | solution.py:357

commit v3 on v2

--- a/solution.py
+++ b/solution.py
@@ -20,30 +20,27 @@
     return [1 << b for b in range(count.bit_length() - 1)]
 
 
-def plan(count):
-    last = count - 1
-    steps = []
-    for s in range(-1, SWEEPS + 1):
-        steps += [("couple", s, 0), ("relay rhs", s - 1, last)]
-        steps += [("relay state", s, 1), ("solve", s - 1, last), ("couple", s, 1)]
-        for c in range(2, count):
-            steps += [("relay state", s, c), ("couple", s, c), ("correct", s, c - 2)]
-        steps += [("relay rhs", s, 0), ("solve", s, 0)]
-        for c in range(1, last):
-            steps += [("correct", s, c + 1), ("relay rhs", s, c)]
-            if c == last - 1:
-                steps += [("relay state", s + 1, 0)]
-            steps += [("solve", s, c)]
-    def holds(step, s, c):
-        if step == "relay state":
-            return 0 <= s < SWEEPS
-        return (-1 if step in ("relay rhs", "solve") else 0) <= s < SWEEPS
-    return [entry for entry in steps if holds(*entry)]
+STEPS = (
+    ("couple near", 0, 0), ("couple mid", 0, 0), ("solve mid", 2, 1), ("solve near", 3, 1),
+    ("couple far", 0, 0), ("solve far", 2, 1), ("couple near", 1, 0), ("couple mid", 1, 0),
+    ("solve mid", 3, 1), ("couple far", 1, 0), ("solve far", 3, 1), ("couple near", 2, 0),
+    ("couple mid", 2, 0), ("couple near", 3, 0), ("couple far", 2, 0), ("correct", 0, 0),
+    ("couple mid", 3, 0), ("couple far", 3, 0), ("correct", 1, 0), ("solve near", 0, 0),
+    ("solve mid", 0, 0), ("solve near", 1, 0), ("solve far", 0, 0), ("correct", 2, 0),
+    ("solve mid", 1, 0), ("solve near", 2, 0), ("solve far", 1, 0), ("correct", 3, 0),
+)
+
+
+def steps_of(count):
+    if count == 4:
+        return STEPS
+    names = ("couple near", "couple mid", "couple far", "correct", "solve near", "solve mid", "solve far")
+    return tuple((name, c, 0) for name in names for c in range(count))
 
 
 def sweep_kernel(
     walls, harms, strip, sketch, inverse, up, down, sampled, gram,
-    sketch_v, pieces, inverse_v, couple_v, partial, halo_out, halo_in,
+    sketch_v, pieces, inverse_v, couple_v, solved, local, away, halo_out, halo_in,
     whole, summed, gathered, gram_out, gram_in,
     load_sem, recv_sem, send_sem, halo_send, halo_recv, gram_send, gram_recv,
 ):
@@ -64,59 +61,71 @@
     greet += [{"harm": prev}, {"harm": following}]
     barrier = pltpu.get_barrier_semaphore()
 
-    own_copy = pltpu.make_async_copy(sketch, sketch_v, load_sem.at[count + 2])
+    own_copy = pltpu.make_async_copy(sketch, sketch_v, load_sem.at[0])
     own_copy.start()
     for peer in greet:
         pl.semaphore_signal(barrier, inc=1, device_id=peer, device_id_type=MESH)
-    inverse_loads = [
-        pltpu.make_async_copy(inverse.at[h], inverse_v.at[h], load_sem.at[h]) for h in range(count)
-    ]
-    couple_loads = [
-        pltpu.make_async_copy(up, couple_v.at[pl.ds(0, BAND)], load_sem.at[count]),
-        pltpu.make_async_copy(down, couple_v.at[pl.ds(BAND, BAND)], load_sem.at[count + 1]),
-    ]
-    for copy in inverse_loads + couple_loads:
-        copy.start()
-
-    def block(g, c, m):
+
+    inverse_loads, couple_loads = [], []
+    for m in range(walls):
         source = w
         for b in wall_bits:
             if m & b:
                 source = flip(source, b)
-        return pieces.at[g, c, pl.ds(pl.multiple_of(source * rows, rows), rows)]
+        there = pl.ds(pl.multiple_of(source * rows, rows), rows)
+        here = pl.ds(m * rows, rows)
+        inverse_loads.append(pltpu.make_async_copy(
+            inverse.at[:, :, there], inverse_v.at[:, :, here], load_sem.at[1 + m]
+        ))
+        for at, matrix in enumerate((up, down)):
+            couple_loads.append(pltpu.make_async_copy(
+                matrix.at[:, :, there], couple_v.at[at, :, :, here],
+                load_sem.at[1 + walls * (1 + at) + m],
+            ))
+    for copy in inverse_loads + couple_loads:
+        copy.start()
 
     def hop(g, c, m, bit):
         return pltpu.make_async_remote_copy(
-            src_ref=block(g, c, m), dst_ref=block(g, c, m),
+            src_ref=pieces.at[g, c, m], dst_ref=pieces.at[g, c, m + bit],
             send_sem=send_sem.at[g, c, m + bit], recv_sem=recv_sem.at[g, c, m + bit],
             device_id={"wall": flip(w, bit)}, device_id_type=MESH,
         )
 
     def arrival(g, c, m):
         low = m & -m
-        return pltpu.make_async_remote_copy(
-            src_ref=block(g, c, m), dst_ref=block(g, c, m),
-            send_sem=send_sem.at[g, c, m], recv_sem=recv_sem.at[g, c, m],
-            device_id={"wall": flip(w, low)}, device_id_type=MESH,
-        )
+        return hop(g, c, m - low, low)
 
     def send_own(g, c):
         for bit in reversed(wall_bits):
             hop(g, c, 0, bit).start()
 
-    def relay(g, c):
-        for m in sorted(range(2, walls, 2), key=lambda m: -(m & -m)):
-            arrival(g, c, m).wait_recv()
-            for bit in reversed(wall_bits):
-                if bit < (m & -m):
-                    hop(g, c, m, bit).start()
-
-    def finish(g, c):
-        for m in range(1, walls, 2):
-            arrival(g, c, m).wait_recv()
-
-    def own(c):
-        return pl.ds(pl.multiple_of(w * rows, rows), rows)
+    relayed = sorted(range(2, walls, 2), key=lambda m: -(m & -m))
+    spans = {
+        "near": [(0, min(2, walls))],
+        "mid": [(m, m + 1) for m in range(2, walls, 2)],
+        "far": [(m, m + 1) for m in range(3, walls, 2)],
+    }
+
+    def collect(part, g, c):
+        if part == "near":
+            if walls > 1:
+                arrival(g, c, 1).wait_recv()
+        elif part == "mid":
+            for m in relayed:
+                arrival(g, c, m).wait_recv()
+                for bit in reversed(wall_bits):
+                    if bit < (m & -m):
+                        hop(g, c, m, bit).start()
+        else:
+            for m in range(3, walls, 2):
+                arrival(g, c, m).wait_recv()
+
+    def times(matrix, g, c, low, high):
+        piece = pieces[g, c, low:high].reshape((high - low) * rows, width)
+        return jnp.dot(
+            matrix[:, low * rows : high * rows], piece, preferred_element_type=jnp.float32
+        )
 
     def halo(s, side, c):
         return pltpu.make_async_remote_copy(
@@ -132,83 +141,94 @@
             source = sketch_v[h].astype(jnp.float32)
             source = source if turn == 0 else pltpu.roll(source, turn, 1)
             tile = source if tile is None else jnp.where(lane < h * lanes, tile, source)
-        pieces[0, c, own(c), :] = tile.astype(jnp.bfloat16)
+        pieces[0, c, 0] = tile.astype(jnp.bfloat16)
         send_own(0, c)
 
     shifts = [(strip[j] + 1) * lanes for j in range(BAND)]
 
-    def couple(s, c):
+    def couple(part, s, c):
         g = 2 * s + 1
-        finish(g, c)
-        local = pieces[0, c, own(c), :].astype(jnp.float32)
-        away = jnp.zeros((rows, width), jnp.float32)
-        for j in range(BAND):
-            product = jnp.dot(couple_v[j], pieces[g, c], preferred_element_type=jnp.float32)
-            product = pltpu.roll(product, lax.rem(shifts[j], width), 1)
-            stays = lane >= shifts[j]
-            local = local - jnp.where(stays, product, 0.0)
-            away = away + jnp.where(stays, 0.0, product)
-        halo_out[s, 1, c] = away.astype(jnp.bfloat16)
-        halo(s, 1, c).start()
-        away = jnp.zeros((rows, width), jnp.float32)
-        for j in range(BAND):
-            product = jnp.dot(couple_v[BAND + j], pieces[g, c], preferred_element_type=jnp.float32)
-            product = pltpu.roll(product, width - shifts[j], 1)
-            stays = lane < width - shifts[j]
-            local = local - jnp.where(stays, product, 0.0)
-            away = away + jnp.where(stays, 0.0, product)
-        halo_out[s, 0, c] = away.astype(jnp.bfloat16)
-        halo(s, 0, c).start()
-        partial[c] = local
+        collect(part, g, c)
+        if part == "near":
+            inner = pieces[0, c, 0].astype(jnp.float32)
+        else:
+            inner = local[c]
+        for side in (1, 0):
+            outer = jnp.zeros((rows, width), jnp.float32) if part == "near" else away[side, c]
+            for j in range(BAND):
+                if side == 1:
+                    turn, stays = lax.rem(shifts[j], width), lane >= shifts[j]
+                else:
+                    turn, stays = width - shifts[j], lane < width - shifts[j]
+                for low, high in spans[part]:
+                    product = times(couple_v.at[1 - side, j], g, c, low, high)
+                    product = pltpu.roll(product, turn, 1)
+                    inner = inner - jnp.where(stays, product, 0.0)
+                    outer = outer + jnp.where(stays, 0.0, product)
+            if part == "far":
+                halo_out[s, side, c] = outer.astype(jnp.bfloat16)
+                halo(s, side, c).start()
+            else:
+                away[side, c] = outer
+        local[c] = inner
 
     def correct(s, c):
-        rhs = partial[c]
+        rhs = local[c]
         for side in (1, 0):
             halo(s, side, c).wait_recv()
             rhs = rhs - halo_in[s, side, c].astype(jnp.float32)
-        pieces[2 * s + 2, c, own(c), :] = rhs.astype(jnp.bfloat16)
+        pieces[2 * s + 2, c, 0] = rhs.astype(jnp.bfloat16)
         send_own(2 * s + 2, c)
 
-    def solve(s, c):
+    def solve(part, s, c):
         g = 2 * s + 2
-        finish(g, c)
-        result = None
-        for h in range(count):
-            product = jnp.dot(inverse_v[h], pieces[g, c], preferred_element_type=jnp.float32)
-            result = product if result is None else jnp.where(lane < h * lanes, result, product)
-        if s < SWEEPS - 1:
-            pieces[g + 1, c, own(c), :] = result.astype(jnp.bfloat16)
-            send_own(g + 1, c)
-        else:
-            partial[c] = result
+        collect(part, g, c)
+        total = None
+        for low, high in spans[part]:
+            result = None
+            for h in range(count):
+                product = times(inverse_v.at[h], g, c, low, high)
+                result = product if result is None else jnp.where(lane < h * lanes, result, product)
+            total = result if total is None else total + result
+        if part != "near":
+            total = solved[c] + total
+        if part == "far":
+            @pl.when(s < SWEEPS - 1)
+            def _():
+                pieces[g + 1, c, 0] = total.astype(jnp.bfloat16)
+                send_own(g + 1, c)
+        solved[c] = total
+
+    def take(steps, s):
+        for name, c, lag in steps:
+            kind, _, part = name.partition(" ")
+            if kind == "couple":
+                couple(part, s, c)
+            elif kind == "correct":
+                correct(s, c)
+            else:
+                solve(part, s - lag, c)
 
     pl.semaphore_wait(barrier, len(greet))
     own_copy.wait()
     for c in range(count):
         start(c)
-    ready = set()
-    for step, s, c in plan(count):
-        if step == "solve" and "inverse" not in ready:
-            ready.add("inverse")
-            for copy in inverse_loads:
-                copy.wait()
-        if step == "couple" and "couple" not in ready:
-            ready.add("couple")
-            for copy in couple_loads:
-                copy.wait()
-        if step == "relay rhs":
-            relay(2 * s + 2, c)
-        elif step == "relay state":
-            relay(2 * s + 1, c)
-        else:
-            {"solve": solve, "couple": couple, "correct": correct}[step](s, c)
+    for copy in inverse_loads:
+        copy.wait()
+    steps = steps_of(count)
+    solves = [step for step in steps if step[0].startswith("solve")]
+    take([step for step in solves if step[2] == 0], -1)
+    for copy in couple_loads:
+        copy.wait()
+    pl.loop(0, SWEEPS)(lambda s: take(steps, s))
+    take([step for step in solves if step[2] == 1], SWEEPS)
 
     total = jnp.zeros((width, width), jnp.float32)
     for h in range(count):
         tile = None
         for c in range(count):
             turn = (c - h) % count * lanes
-            source = partial[c] if turn == 0 else pltpu.roll(partial[c], turn, 1)
+            source = solved[c] if turn == 0 else pltpu.roll(solved[c], turn, 1)
             tile = source if tile is None else jnp.where(lane < c * lanes, tile, source)
         sampled[h] = tile
         total = total + lax.dot_general(
@@ -255,11 +275,16 @@
     summed[place, :] = half
     swap(stage, summed.at[place], summed.at[place], {"wall": flip(w, 1)}).wait()
     gram[...] = summed[...]
-    for c in range(count):
-        for g in range(2 * SWEEPS + 1):
+
+    @pl.loop(0, 2 * SWEEPS + 1)
+    def _(g):
+        for c in range(count):
             for m in range(1, walls):
                 arrival(g, c, m).wait_send()
-        for s in range(SWEEPS):
+
+    @pl.loop(0, SWEEPS)
+    def _(s):
+        for c in range(count):
             for side in range(2):
                 halo(s, side, c).wait_send()
 
@@ -330,10 +355,12 @@
         out_specs=(vmem, vmem),
         scratch_shapes=[
             pltpu.VMEM((count, rows, width), jnp.bfloat16),
-            pltpu.VMEM((gathers, count, size, width), jnp.bfloat16),
+            pltpu.VMEM((gathers, count, walls, rows, width), jnp.bfloat16),
             pltpu.VMEM((count, rows, size), jnp.bfloat16),
-            pltpu.VMEM((2 * BAND, rows, size), jnp.bfloat16),
+            pltpu.VMEM((2, BAND, rows, size), jnp.bfloat16),
             pltpu.VMEM((count, rows, width), jnp.float32),
+            pltpu.VMEM((count, rows, width), jnp.float32),
+            pltpu.VMEM((2, count, rows, width), jnp.float32),
             pltpu.VMEM((SWEEPS, 2, count, rows, width), jnp.bfloat16),
             pltpu.VMEM((SWEEPS, 2, count, rows, width), jnp.bfloat16),
             pltpu.VMEM((width, width), jnp.float32),
@@ -341,7 +368,7 @@
             pltpu.VMEM((near, width // 2, width), jnp.float32),
             pltpu.VMEM((stages, width // 2, width), jnp.float32),
             pltpu.VMEM((stages, width // 2, width), jnp.float32),
-            pltpu.SemaphoreType.DMA((count + 3,)),
+            pltpu.SemaphoreType.DMA((1 + 3 * walls,)),
             pltpu.SemaphoreType.DMA((gathers, count, walls)),
             pltpu.SemaphoreType.DMA((gathers, count, walls)),
             pltpu.SemaphoreType.DMA((SWEEPS, 2, count)),

time: 99.1 us -> 94.7 us (0.956)
  Pallas kernels: 98.3 us -> 93.9 us
    pallas_call x1, Pallas kernels: 87.5 us -> 83 us  [body(): pl.pallas_call(functools.partial(sweep_kernel, walls, harms), out_shape=(...]
where the time goes in v3:
time: 94.7 us; the launch traced here: 94.5 us
  Pallas kernels  93.9 us (99%)
    pallas_call x1, Pallas kernels, body(): pl.pallas_call(functools.partial(sweep_kernel, walls, harms), out_shape=(...  83 us
    pallas_call x1, Pallas kernels, body(): pl.pallas_call(factor_kernel, out_shape=(jax.ShapeDtypeStruct((count, row...  10.9 us

profile of v3, /device:TPU:0, one launch (start us, length us, event | category | flops | bytes accessed | tf_op | source)
XLA Modules:
  0.0 94.5 jit_solution(3746032706282522806)
XLA Ops:
  0.6 83.0 %sweeps.1 = (f32[4,256,128]{2,1,0:T(8,128)}, f32[128,128]{1,0:T(8,128)}) custom-call(s32[4]{0:T(128)} %strip.1, bf16[4,256,128]{2,1,0:T(8,128)(2,1)} %sketch.1, bf16[4,256,1024]{2,1,0:T(8,128)(2,1)} %inverse.1, bf16[4,256,1024]{2,1,0:T(8,128)(2,1)} %up.1, bf16[4,256,1024]{2,1,0:T(8,128)(2,1)} %down.1), custom_call_target="tpu_custom_call" | custom-call | tf_op jit(solution)/shard_map/sweeps/pallas_call | solution.py:348
  83.7 10.9 %factor.1 = (f32[4,256,128]{2,1,0:T(8,128)}, f32[128,128]{1,0:T(8,128)}) custom-call(f32[4,256,128]{2,1,0:T(8,128)} %get-tuple-element.4.sampled, f32[128,128]{1,0:T(8,128)} %get-tuple-element.5.gram), custom_call_target="tpu_custom_call" | custom-call | tf_op jit(solution)/shard_map/factor/pallas_call | solution.py:384

commit v4 on v3

--- a/solution.py
+++ b/solution.py
@@ -39,8 +39,8 @@
 
 
 def sweep_kernel(
-    walls, harms, strip, sketch, inverse, up, down, sampled, gram,
-    sketch_v, pieces, inverse_v, couple_v, solved, local, away, halo_out, halo_in,
+    walls, harms, strip_in, sketch, inverse, up, down, sampled, gram,
+    strip, sampled_v, sketch_v, pieces, inverse_v, couple_v, solved, local, away, halo_out, halo_in,
     whole, summed, gathered, gram_out, gram_in,
     load_sem, recv_sem, send_sem, halo_send, halo_recv, gram_send, gram_recv,
 ):
@@ -63,6 +63,8 @@
 
     own_copy = pltpu.make_async_copy(sketch, sketch_v, load_sem.at[0])
     own_copy.start()
+    strip_copy = pltpu.make_async_copy(strip_in, strip, load_sem.at[1 + 3 * walls])
+    strip_copy.start()
     for peer in greet:
         pl.semaphore_signal(barrier, inc=1, device_id=peer, device_id_type=MESH)
 
@@ -144,8 +146,6 @@
         pieces[0, c, 0] = tile.astype(jnp.bfloat16)
         send_own(0, c)
 
-    shifts = [(strip[j] + 1) * lanes for j in range(BAND)]
-
     def couple(part, s, c):
         g = 2 * s + 1
         collect(part, g, c)
@@ -153,6 +153,7 @@
             inner = pieces[0, c, 0].astype(jnp.float32)
         else:
             inner = local[c]
+        shifts = [(strip[j] + 1) * lanes for j in range(BAND)]
         for side in (1, 0):
             outer = jnp.zeros((rows, width), jnp.float32) if part == "near" else away[side, c]
             for j in range(BAND):
@@ -213,6 +214,7 @@
     own_copy.wait()
     for c in range(count):
         start(c)
+    strip_copy.wait()
     for copy in inverse_loads:
         copy.wait()
     steps = steps_of(count)
@@ -223,6 +225,10 @@
     pl.loop(0, SWEEPS)(lambda s: take(steps, s))
     take([step for step in solves if step[2] == 1], SWEEPS)
 
+    out_copies = [
+        pltpu.make_async_copy(sampled_v.at[h], sampled.at[h], load_sem.at[2 + 3 * walls + h])
+        for h in range(count)
+    ]
     total = jnp.zeros((width, width), jnp.float32)
     for h in range(count):
         tile = None
@@ -230,7 +236,8 @@
             turn = (c - h) % count * lanes
             source = solved[c] if turn == 0 else pltpu.roll(solved[c], turn, 1)
             tile = source if tile is None else jnp.where(lane < c * lanes, tile, source)
-        sampled[h] = tile
+        sampled_v[h] = tile
+        out_copies[h].start()
         total = total + lax.dot_general(
             tile, tile, (((0,), (0,)), ((), ())),
             precision=lax.Precision.HIGHEST, preferred_element_type=jnp.float32,
@@ -276,6 +283,9 @@
     swap(stage, summed.at[place], summed.at[place], {"wall": flip(w, 1)}).wait()
     gram[...] = summed[...]
 
+    for copy in out_copies:
+        copy.wait()
+
     @pl.loop(0, 2 * SWEEPS + 1)
     def _(g):
         for c in range(count):
@@ -289,9 +299,15 @@
                 halo(s, side, c).wait_send()
 
 
-def factor_kernel(sampled, gram, basis, triangle, work, inverse_lower):
-    count, rows, width = sampled.shape
-    panel = 8
+def factor_kernel(sampled, gram, basis, triangle, sampled_v, basis_v, work, inverse_lower, sems):
+    count, rows, width = sampled_v.shape
+    panel, block = 32, 16
+    loads = [
+        pltpu.make_async_copy(sampled.at[h], sampled_v.at[h], sems.at[0, h]) for h in range(count)
+    ]
+    stores = [pltpu.make_async_copy(basis_v.at[h], basis.at[h], sems.at[1, h]) for h in range(count)]
+    for copy in loads:
+        copy.start()
     row_at = lax.broadcasted_iota(jnp.int32, (width, width), 0)
     col_at = lax.broadcasted_iota(jnp.int32, (width, width), 1)
     at = lax.broadcasted_iota(jnp.int32, (panel, width), 0)
@@ -304,18 +320,20 @@
     for low in range(0, width, panel):
         a = work[low : low + panel, :]
         x = inverse_lower[low : low + panel, :]
-        columns = [
-            jnp.broadcast_to(a[:, low + i : low + i + 1], (panel, width)) for i in range(panel)
-        ]
         pivots = jnp.ones((panel, width), jnp.float32)
-        for i in range(panel):
-            pivot = spread(columns[i], i)
-            pivots = jnp.where(at == i, pivot, pivots)
-            factor = jnp.where(at > i, columns[i] * (1.0 / pivot), 0.0)
-            for m in range(i + 1, panel):
-                columns[m] = columns[m] - factor * spread(columns[m], i)
-            a = a - factor * spread(a, i)
-            x = x - factor * spread(x, i)
+        for first in range(0, panel, block):
+            columns = {
+                i: jnp.broadcast_to(a[:, low + i : low + i + 1], (panel, width))
+                for i in range(first, first + block)
+            }
+            for i in range(first, first + block):
+                pivot = spread(columns[i], i)
+                pivots = jnp.where(at == i, pivot, pivots)
+                factor = jnp.where(at > i, columns[i] * (1.0 / pivot), 0.0)
+                for m in range(i + 1, first + block):
+                    columns[m] = columns[m] - factor * spread(columns[m], i)
+                a = a - factor * spread(a, i)
+                x = x - factor * spread(x, i)
         unit = lax.rsqrt(pivots)
         a, x = a * unit, x * unit
         work[low : low + panel, :] = a
@@ -329,12 +347,16 @@
             work[below:, :] = work[below:, :] - change[below:, :width]
             inverse_lower[below:, :] = inverse_lower[below:, :] - change[below:, width:]
 
+    for h in range(count):
+        loads[h].wait()
+        basis_v[h] = lax.dot_general(
+            sampled_v[h], inverse_lower[...], (((1,), (1,)), ((), ())),
+            precision=lax.Precision.HIGHEST, preferred_element_type=jnp.float32,
+        )
+        stores[h].start()
     triangle[...] = jnp.where(row_at <= col_at, work[...], 0.0)
-    for h in range(count):
-        basis[h] = lax.dot_general(
-            sampled[h], inverse_lower[...], (((1,), (1,)), ((), ())),
-            precision=lax.Precision.HIGHEST, preferred_element_type=jnp.float32,
-        )
+    for copy in stores:
+        copy.wait()
 
 
 def body(walls, harms, sketch, inverse_blocks, couple_up, couple_down, strip_harmonics):
@@ -351,9 +373,11 @@
             jax.ShapeDtypeStruct((count, rows, width), jnp.float32),
             jax.ShapeDtypeStruct((width, width), jnp.float32),
         ),
-        in_specs=[pl.BlockSpec(memory_space=pltpu.SMEM)] + [anywhere] * 4,
-        out_specs=(vmem, vmem),
+        in_specs=[anywhere] * 5,
+        out_specs=(anywhere, vmem),
         scratch_shapes=[
+            pltpu.SMEM((BAND,), jnp.int32),
+            pltpu.VMEM((count, rows, width), jnp.float32),
             pltpu.VMEM((count, rows, width), jnp.bfloat16),
             pltpu.VMEM((gathers, count, walls, rows, width), jnp.bfloat16),
             pltpu.VMEM((count, rows, size), jnp.bfloat16),
@@ -368,7 +392,7 @@
             pltpu.VMEM((near, width // 2, width), jnp.float32),
             pltpu.VMEM((stages, width // 2, width), jnp.float32),
             pltpu.VMEM((stages, width // 2, width), jnp.float32),
-            pltpu.SemaphoreType.DMA((1 + 3 * walls,)),
+            pltpu.SemaphoreType.DMA((2 + 3 * walls + count,)),
             pltpu.SemaphoreType.DMA((gathers, count, walls)),
             pltpu.SemaphoreType.DMA((gathers, count, walls)),
             pltpu.SemaphoreType.DMA((SWEEPS, 2, count)),
@@ -387,9 +411,15 @@
             jax.ShapeDtypeStruct((count, rows, width), jnp.float32),
             jax.ShapeDtypeStruct((width, width), jnp.float32),
         ),
-        in_specs=[vmem, vmem],
-        out_specs=(vmem, vmem),
-        scratch_shapes=[pltpu.VMEM((width, width), jnp.float32)] * 2,
+        in_specs=[anywhere, vmem],
+        out_specs=(anywhere, vmem),
+        scratch_shapes=[
+            pltpu.VMEM((count, rows, width), jnp.float32),
+            pltpu.VMEM((count, rows, width), jnp.float32),
+            pltpu.VMEM((width, width), jnp.float32),
+            pltpu.VMEM((width, width), jnp.float32),
+            pltpu.SemaphoreType.DMA((2, count)),
+        ],
         name="factor",
     )(sampled, gram)
 

time: 94.7 us -> 91 us (0.961)
  Pallas kernels: 93.9 us -> 90 us
    pallas_call x1, Pallas kernels: 10.9 us -> 7.73 us  [body(): pl.pallas_call(factor_kernel, out_shape=(jax.ShapeDtypeStruct((count, row...]
where the time goes in v4:
time: 91 us; the launch traced here: 90.8 us
  Pallas kernels  90 us (99%)
    pallas_call x1, Pallas kernels, body(): pl.pallas_call(functools.partial(sweep_kernel, walls, harms), out_shape=(...  82.3 us
    pallas_call x1, Pallas kernels, body(): pl.pallas_call(factor_kernel, out_shape=(jax.ShapeDtypeStruct((count, row...  7.73 us

profile of v4, /device:TPU:0, one launch (start us, length us, event | category | flops | bytes accessed | tf_op | source)
XLA Modules:
  0.0 90.8 jit_solution(11550013834212418839)
XLA Ops:
  0.6 82.3 %sweeps.1 = (f32[4,256,128]{2,1,0:T(8,128)}, f32[128,128]{1,0:T(8,128)}) custom-call(s32[4]{0:T(128)} %strip_in.1, bf16[4,256,128]{2,1,0:T(8,128)(2,1)} %sketch.1, bf16[4,256,1024]{2,1,0:T(8,128)(2,1)} %inverse.1, bf16[4,256,1024]{2,1,0:T(8,128)(2,1)} %up.1, bf16[4,256,1024]{2,1,0:T(8,128)(2,1)} %down.1), custom_call_target="tpu_custom_call" | custom-call | tf_op jit(solution)/shard_map/sweeps/pallas_call | solution.py:370
  82.9 7.7 %factor.1 = (f32[4,256,128]{2,1,0:T(8,128)}, f32[128,128]{1,0:T(8,128)}) custom-call(f32[4,256,128]{2,1,0:T(8,128)} %get-tuple-element.4.sampled, f32[128,128]{1,0:T(8,128)} %get-tuple-element.5.gram), custom_call_target="tpu_custom_call" | custom-call | tf_op jit(solution)/shard_map/factor/pallas_call | solution.py:408

commit v5 on v4

--- a/solution.py
+++ b/solution.py
@@ -38,10 +38,42 @@
     return tuple((name, c, 0) for name in names for c in range(count))
 
 
+def pack(full, packed):
+    width = full.shape[0]
+    part, quarter = width // 2, width // 4
+    row = lax.broadcasted_iota(jnp.int32, (part, width), 0)
+    lane = lax.broadcasted_iota(jnp.int32, (part, width), 1)
+    left = lane[:quarter] < part
+    top, low = full[:part], pltpu.roll(full[part:], part, 1)
+    turned = pltpu.roll(top, part, 1)
+    packed[0, :quarter] = jnp.where(left, turned[:quarter], top[quarter:])
+    mixed = jnp.where(row <= lane, top, low)
+    packed[1, :quarter] = jnp.where(left, mixed[:quarter], pltpu.roll(mixed[quarter:], part, 1))
+    diagonal = jnp.sum(jnp.where(row == lane, low, 0.0), axis=0, keepdims=True)
+    packed[0, quarter:] = jnp.zeros((8, width), jnp.float32)
+    packed[1, quarter:] = jnp.broadcast_to(diagonal, (8, width))
+
+
+def unpack(packed, width):
+    part, quarter = width // 2, width // 4
+    row = lax.broadcasted_iota(jnp.int32, (part, width), 0)
+    lane = lax.broadcasted_iota(jnp.int32, (part, width), 1)
+    cross, mixed = packed[0, :quarter], packed[1, :quarter]
+    cross = jnp.concatenate([pltpu.roll(cross, part, 1), cross], axis=0)
+    mixed = jnp.concatenate([mixed, pltpu.roll(mixed, part, 1)], axis=0)
+    diagonal = jnp.broadcast_to(packed[1, quarter : quarter + 1], (part, width))
+    top = jnp.where(lane < part, jnp.where(row <= lane, mixed, 0.0), cross)
+    low = jnp.where(row > lane, mixed, jnp.where(row == lane, diagonal, 0.0))
+    once = jnp.concatenate([top, pltpu.roll(low, part, 1)], axis=0)
+    row = lax.broadcasted_iota(jnp.int32, (width, width), 0)
+    lane = lax.broadcasted_iota(jnp.int32, (width, width), 1)
+    return jnp.where(row == lane, once, once + once.T)
+
+
 def sweep_kernel(
     walls, harms, strip_in, sketch, inverse, up, down, sampled, gram,
     strip, sampled_v, sketch_v, pieces, inverse_v, couple_v, solved, local, away, halo_out, halo_in,
-    whole, summed, gathered, gram_out, gram_in,
+    packed, summed, gathered, gram_out, gram_in,
     load_sem, recv_sem, send_sem, halo_send, halo_recv, gram_send, gram_recv,
 ):
     count, rows, width = sketch.shape
@@ -53,12 +85,17 @@
     lane = lax.broadcasted_iota(jnp.int32, (rows, width), 1)
 
     near = min(4, harms)
-    butterfly = [("wall", flip(w, b)) for b in wall_bits if b > 1]
+    butterfly = [("wall", flip(w, b)) for b in wall_bits if b > 2]
     butterfly += [("harm", flip(z, b)) for b in harm_bits if b >= near]
     greet = [{"wall": flip(w, b)} for b in wall_bits]
     greet += [{"harm": flip(z, b)} for b in harm_bits if b >= near]
-    greet += [{"harm": z - z % near + (z % near + d) % near} for d in range(1, near)]
     greet += [{"harm": prev}, {"harm": following}]
+    direct = []
+    for across in range(2):
+        for d in range(near):
+            peer = {"harm": z - z % near + (z % near + d) % near} if d else {}
+            peer.update({"wall": flip(w, 2)} if across else {})
+            direct += [peer] if peer else []
     barrier = pltpu.get_barrier_semaphore()
 
     own_copy = pltpu.make_async_copy(sketch, sketch_v, load_sem.at[0])
@@ -144,7 +181,6 @@
             source = source if turn == 0 else pltpu.roll(source, turn, 1)
             tile = source if tile is None else jnp.where(lane < h * lanes, tile, source)
         pieces[0, c, 0] = tile.astype(jnp.bfloat16)
-        send_own(0, c)
 
     def couple(part, s, c):
         g = 2 * s + 1
@@ -210,10 +246,12 @@
             else:
                 solve(part, s - lag, c)
 
-    pl.semaphore_wait(barrier, len(greet))
     own_copy.wait()
     for c in range(count):
         start(c)
+    pl.semaphore_wait(barrier, len(greet))
+    for c in range(count):
+        send_own(0, c)
     strip_copy.wait()
     for copy in inverse_loads:
         copy.wait()
@@ -243,9 +281,6 @@
             precision=lax.Precision.HIGHEST, preferred_element_type=jnp.float32,
         )
 
-    part = width // 2
-    mine, theirs = (w % 2) * part, (1 - w % 2) * part
-
     def swap(stage, source, target, peer):
         copy = pltpu.make_async_remote_copy(
             src_ref=source, dst_ref=target, send_sem=gram_send.at[stage],
@@ -254,34 +289,31 @@
         copy.start()
         return copy
 
-    whole[...] = total
-    swap(
-        0, whole.at[pl.ds(pl.multiple_of(theirs, part), part)], gram_in.at[0], {"wall": flip(w, 1)}
-    ).wait()
-    half = whole[pl.ds(pl.multiple_of(mine, part), part), :] + gram_in[0]
+    side = w % 2
+    pack(total, packed)
+    swap(0, packed.at[1 - side], gram_in.at[0], {"wall": flip(w, 1)}).wait()
+    half = packed[side] + gram_in[0]
     stage = 1
     for axis, peer in butterfly:
         gram_out[stage] = half
         swap(stage, gram_out.at[stage], gram_in.at[stage], {axis: peer}).wait()
         half = half + gram_in[stage]
         stage += 1
-    me = z % near
+    me = lax.div(w, 2) % 2 * near + z % near
     gathered[me] = half
     copies = [
-        swap(stage + d - 1, gathered.at[me], gathered.at[me], {"harm": z - me + (me + d) % near})
-        for d in range(1, near)
+        swap(stage + at, gathered.at[me], gathered.at[me], peer)
+        for at, peer in enumerate(direct)
     ]
     for copy in copies:
         copy.wait()
     half = gathered[0]
-    for d in range(1, near):
-        half = half + gathered[d]
-    stage += near - 1
-    half = half / (harms * walls * count * rows)
-    place = pl.ds(pl.multiple_of(mine, part), part)
-    summed[place, :] = half
-    swap(stage, summed.at[place], summed.at[place], {"wall": flip(w, 1)}).wait()
-    gram[...] = summed[...]
+    for slot in range(1, len(direct) + 1):
+        half = half + gathered[slot]
+    stage += len(direct)
+    summed[side] = half / (harms * walls * count * rows)
+    swap(stage, summed.at[side], summed.at[side], {"wall": flip(w, 1)}).wait()
+    gram[...] = unpack(summed, width)
 
     for copy in out_copies:
         copy.wait()
@@ -363,7 +395,8 @@
     count, rows, width = sketch.shape
     size = rows * walls
     near = min(4, harms)
-    stages = len(bits_of(walls)) + len(bits_of(harms // near)) + near
+    stages = len(bits_of(walls)) + len(bits_of(harms // near)) + 2 * near
+    short = width // 4 + 8
     gathers = 1 + 2 * SWEEPS
     vmem = pl.BlockSpec(memory_space=pltpu.VMEM)
     anywhere = pl.BlockSpec(memory_space=pl.ANY)
@@ -387,11 +420,11 @@
             pltpu.VMEM((2, count, rows, width), jnp.float32),
             pltpu.VMEM((SWEEPS, 2, count, rows, width), jnp.bfloat16),
             pltpu.VMEM((SWEEPS, 2, count, rows, width), jnp.bfloat16),
-            pltpu.VMEM((width, width), jnp.float32),
-            pltpu.VMEM((width, width), jnp.float32),
-            pltpu.VMEM((near, width // 2, width), jnp.float32),
-            pltpu.VMEM((stages, width // 2, width), jnp.float32),
-            pltpu.VMEM((stages, width // 2, width), jnp.float32),
+            pltpu.VMEM((2, short, width), jnp.float32),
+            pltpu.VMEM((2, short, width), jnp.float32),
+            pltpu.VMEM((2 * near, short, width), jnp.float32),
+            pltpu.VMEM((stages, short, width), jnp.float32),
+            pltpu.VMEM((stages, short, width), jnp.float32),
             pltpu.SemaphoreType.DMA((2 + 3 * walls + count,)),
             pltpu.SemaphoreType.DMA((gathers, count, walls)),
             pltpu.SemaphoreType.DMA((gathers, count, walls)),

time: 91 us -> 90.1 us (level)
  no operation moved by 1% of the time
where the time goes in v5:
time: 90.1 us; the launch traced here: 89.9 us
  Pallas kernels  89.1 us (99%)
    pallas_call x1, Pallas kernels, body(): pl.pallas_call(functools.partial(sweep_kernel, walls, harms), out_shape=(...  81.4 us
    pallas_call x1, Pallas kernels, body(): pl.pallas_call(factor_kernel, out_shape=(jax.ShapeDtypeStruct((count, row...  7.73 us

profile of v5, /device:TPU:0, one launch (start us, length us, event | category | flops | bytes accessed | tf_op | source)
XLA Modules:
  0.0 89.9 jit_solution(15153686837291687216)
XLA Ops:
  0.6 81.4 %sweeps.1 = (f32[4,256,128]{2,1,0:T(8,128)}, f32[128,128]{1,0:T(8,128)}) custom-call(s32[4]{0:T(128)} %strip_in.1, bf16[4,256,128]{2,1,0:T(8,128)(2,1)} %sketch.1, bf16[4,256,1024]{2,1,0:T(8,128)(2,1)} %inverse.1, bf16[4,256,1024]{2,1,0:T(8,128)(2,1)} %up.1, bf16[4,256,1024]{2,1,0:T(8,128)(2,1)} %down.1), custom_call_target="tpu_custom_call" | custom-call | tf_op jit(solution)/shard_map/sweeps/pallas_call | solution.py:403
  82.0 7.7 %factor.1 = (f32[4,256,128]{2,1,0:T(8,128)}, f32[128,128]{1,0:T(8,128)}) custom-call(f32[4,256,128]{2,1,0:T(8,128)} %get-tuple-element.4.sampled, f32[128,128]{1,0:T(8,128)} %get-tuple-element.5.gram), custom_call_target="tpu_custom_call" | custom-call | tf_op jit(solution)/shard_map/factor/pallas_call | solution.py:441

commit v6 on v5

--- a/solution.py
+++ b/solution.py
@@ -74,7 +74,7 @@
     walls, harms, strip_in, sketch, inverse, up, down, sampled, gram,
     strip, sampled_v, sketch_v, pieces, inverse_v, couple_v, solved, local, away, halo_out, halo_in,
     packed, summed, gathered, gram_out, gram_in,
-    load_sem, recv_sem, send_sem, halo_send, halo_recv, gram_send, gram_recv,
+    load_sem, recv_sem, send_sem, halo_send, halo_recv, gram_send, gram_recv, word,
 ):
     count, rows, width = sketch.shape
     lanes = width // count
@@ -89,7 +89,8 @@
     butterfly += [("harm", flip(z, b)) for b in harm_bits if b >= near]
     greet = [{"wall": flip(w, b)} for b in wall_bits]
     greet += [{"harm": flip(z, b)} for b in harm_bits if b >= near]
-    greet += [{"harm": prev}, {"harm": following}]
+    if harms < 3:
+        greet += [{"harm": prev}, {"harm": following}]
     direct = []
     for across in range(2):
         for d in range(near):
@@ -104,6 +105,35 @@
     strip_copy.start()
     for peer in greet:
         pl.semaphore_signal(barrier, inc=1, device_id=peer, device_id_type=MESH)
+
+    def tell(semaphore, peer):
+        pl.semaphore_signal(semaphore, inc=1, device_id={"harm": peer}, device_id_type=MESH)
+
+    heard = len(greet)
+    if harms > 2:
+        pl.when(z > 0)(lambda: tell(barrier, prev))
+        pl.when(z < harms - 1)(lambda: tell(barrier, following))
+        heard = heard + (z > 0).astype(jnp.int32) + (z < harms - 1).astype(jnp.int32)
+
+    def first_word():
+        pl.when(z == 1)(lambda: tell(word.at[0], following))
+        pl.when(z == harms - 2)(lambda: tell(word.at[1], prev))
+
+    def pass_on():
+        @pl.when((z > 1) & (z < harms - 1))
+        def _():
+            pl.semaphore_wait(word.at[0], 1)
+            tell(word.at[0], following)
+
+        @pl.when((z > 0) & (z < harms - 2))
+        def _():
+            pl.semaphore_wait(word.at[1], 1)
+            tell(word.at[1], prev)
+
+    def last_word():
+        pl.when(z == harms - 1)(lambda: pl.semaphore_wait(word.at[0], 1))
+        pl.when(z == 0)(lambda: pl.semaphore_wait(word.at[1], 1))
+
 
     inverse_loads, couple_loads = [], []
     for m in range(walls):
@@ -249,17 +279,23 @@
     own_copy.wait()
     for c in range(count):
         start(c)
-    pl.semaphore_wait(barrier, len(greet))
+    pl.semaphore_wait(barrier, heard)
     for c in range(count):
         send_own(0, c)
+    if harms > 2:
+        first_word()
     strip_copy.wait()
     for copy in inverse_loads:
         copy.wait()
+    if harms > 2:
+        pass_on()
     steps = steps_of(count)
     solves = [step for step in steps if step[0].startswith("solve")]
     take([step for step in solves if step[2] == 0], -1)
     for copy in couple_loads:
         copy.wait()
+    if harms > 2:
+        last_word()
     pl.loop(0, SWEEPS)(lambda s: take(steps, s))
     take([step for step in solves if step[2] == 1], SWEEPS)
 
@@ -432,6 +468,7 @@
             pltpu.SemaphoreType.DMA((SWEEPS, 2, count)),
             pltpu.SemaphoreType.DMA((stages,)),
             pltpu.SemaphoreType.DMA((stages,)),
+            pltpu.SemaphoreType.REGULAR((2,)),
         ],
         compiler_params=pltpu.CompilerParams(
             collective_id=0, has_side_effects=True, vmem_limit_bytes=67043328

time: 90.1 us -> 89.4 us (level)
  no operation moved by 1% of the time
where the time goes in v6:
time: 89.4 us; the launch traced here: 89.3 us
  Pallas kernels  88.4 us (99%)
    pallas_call x1, Pallas kernels, body(): pl.pallas_call(functools.partial(sweep_kernel, walls, harms), out_shape=(...  80.7 us
    pallas_call x1, Pallas kernels, body(): pl.pallas_call(factor_kernel, out_shape=(jax.ShapeDtypeStruct((count, row...  7.74 us

profile of v6, /device:TPU:0, one launch (start us, length us, event | category | flops | bytes accessed | tf_op | source)
XLA Modules:
  0.0 89.3 jit_solution(706786957451986404)
XLA Ops:
  0.6 80.7 %sweeps.1 = (f32[4,256,128]{2,1,0:T(8,128)}, f32[128,128]{1,0:T(8,128)}) custom-call(s32[4]{0:T(128)} %strip_in.1, bf16[4,256,128]{2,1,0:T(8,128)(2,1)} %sketch.1, bf16[4,256,1024]{2,1,0:T(8,128)(2,1)} %inverse.1, bf16[4,256,1024]{2,1,0:T(8,128)(2,1)} %up.1, bf16[4,256,1024]{2,1,0:T(8,128)(2,1)} %down.1), custom_call_target="tpu_custom_call" | custom-call | tf_op jit(solution)/shard_map/sweeps/pallas_call | solution.py:439
  81.3 7.7 %factor.1 = (f32[4,256,128]{2,1,0:T(8,128)}, f32[128,128]{1,0:T(8,128)}) custom-call(f32[4,256,128]{2,1,0:T(8,128)} %get-tuple-element.4.sampled, f32[128,128]{1,0:T(8,128)} %get-tuple-element.5.gram), custom_call_target="tpu_custom_call" | custom-call | tf_op jit(solution)/shard_map/factor/pallas_call | solution.py:478
